TPU v7x, 128 devices: a whole 4x4x4 slice. The times are simulated.
128 devices in a mesh: expert: 32 (over z, y, core), helper: 4 (over x).
Axes of the slice: x: 4, y: 4, z: 4, core: 2. Of those that a mesh axis runs over, the one named last changes fastest.
Arguments:
- tokens: bfloat16 [131072, 768], P(('expert', 'helper')), may hold values from -6 to 6
- gate: float32 [131072], P(('expert', 'helper')), may hold values from 0.2 to 1
- expert_ids: int32 [131072, 1], P(('expert', 'helper')), may hold values from 0 to 127; in each aligned block of 1024 rows (0 to 1023, 1024 to 2047, ...) at most 12 rows name the same one
- backup_ids: int32 [131072, 1], P(('expert', 'helper')), may hold values from 0 to 127; in each aligned block of 1024 rows (0 to 1023, 1024 to 2047, ...) at most 12 rows name the same one
- capacity: int32 [128], replicated, may hold values from 2 to 12
- w_in: bfloat16 [128, 768, 3072], P('expert', None, 'helper'), may hold values from -0.21875 to 0.21875
- w_out: bfloat16 [128, 3072, 768], P('expert', 'helper'), may hold values from -0.109375 to 0.109375
Outputs:
- mixed: bfloat16 [131072, 768], P(('expert', 'helper'))
Inputs may be any that keep to these rules, and one draw needn't show every extreme that they name: `expert_ids`: in the rows of one device no expert is the first expert of more than 12 rows; some expert reaches 12. `backup_ids`: in the rows of one device no expert is the backup of more than 12 rows; some expert reaches 12.
All inputs are finite; a program needn't handle non-finite values.
Results may differ from a plain program's by a relative error of at most 0.0095.
Values may be sent and summed in bfloat16 or wider, within the bound.
No kernel may reach another device: no remote copies, remote signals or barrier semaphores. Data moves between devices by JAX's collectives and lax.ppermute only.
A program may use at most 192 MiB of HBM per device.

v0:
```python
import jax
import jax.numpy as jnp
from jax import lax
from jax.sharding import Mesh
from jax.sharding import PartitionSpec as P

EXPERT = ("expert_0", "expert_1", "expert_2")
EXPERT_HELPER = ("expert_0", "expert_1", "expert_2", "helper")


def split_up(array, dim, size):
    dims = array.shape
    parts = array.reshape(*dims[:dim], size, dims[dim] // size, *dims[dim + 1 :])
    return jnp.moveaxis(parts, dim, 0)


def laid_out(parts, dim):
    parts = jnp.moveaxis(parts, 0, dim)
    dims = parts.shape
    return parts.reshape(*dims[:dim], dims[dim] * dims[dim + 1], *dims[dim + 2 :])


def exchange_in_order(parts, axes, order):
    dims = [lax.axis_size(a) for a in axes]
    parts = parts.reshape(*dims, *parts.shape[1:])
    for k in order:
        parts = lax.all_to_all(parts, axes[k], split_axis=k, concat_axis=k, tiled=True)
    return parts.reshape(-1, *parts.shape[len(axes) :])


def core_and_chips(array, groups, order, split_dim, concat_dim):
    size = lax.axis_size(groups[0]) * lax.axis_size(groups[1])
    parts = split_up(array, split_dim, size)
    return laid_out(exchange_in_order(parts, groups, order), concat_dim)


def assign(first, backup, capacity, count, slot):
    columns = jnp.arange(count, dtype=jnp.int32)
    onehot = (first[:, None] == columns[None, :]).astype(jnp.int32)
    rank = jnp.sum((jnp.cumsum(onehot, axis=0) - onehot) * onehot, axis=1)
    limit = jnp.sum(onehot * capacity[None, :], axis=1)
    kept = rank < limit
    spill = (backup[:, None] == columns[None, :]).astype(jnp.int32) * (1 - kept.astype(jnp.int32))[
        :, None
    ]
    spill_rank = jnp.sum((jnp.cumsum(spill, axis=0) - spill) * spill, axis=1)
    final = jnp.where(kept, first, backup)
    slots = jnp.where(kept, rank, slot + spill_rank)
    return (slots, final)


def quarter_term(rows, weight_in, weight_out):
    hidden = jax.nn.relu(jnp.dot(rows, weight_in, preferred_element_type=jnp.float32)).astype(
        jnp.bfloat16
    )
    return jnp.dot(hidden, weight_out, preferred_element_type=jnp.float32)


def on_device(tokens, gate, expert_ids, backup_ids, capacity, w_in, w_out):
    held = w_in.shape[0]
    experts = held * lax.axis_size(EXPERT)
    helpers = lax.axis_size("helper")
    slot = max(6, 3 * tokens.shape[0] // (2 * experts))
    slots, final = assign(expert_ids[:, 0], backup_ids[:, 0], capacity, experts, slot)
    buffer = (
        jnp.zeros((2 * slot, experts, tokens.shape[1]), jnp.bfloat16).at[slots, final].set(tokens)
    )
    arrived = core_and_chips(buffer, (("expert_0", "expert_1"), "expert_2"), (1, 0), 1, 0)
    whole_in, whole_out = (
        lax.all_gather(w_in, "helper", axis=2, tiled=True),
        lax.all_gather(w_out, "helper", axis=1, tiled=True),
    )
    width = whole_in.shape[2] // helpers
    outputs = []
    for expert in range(held):
        total = jnp.zeros((arrived.shape[0], arrived.shape[2]), jnp.float32)
        for quarter in range(helpers):
            part = quarter_term(
                arrived[:, expert],
                whole_in[expert, :, quarter * width : (quarter + 1) * width],
                whole_out[expert, quarter * width : (quarter + 1) * width, :],
            )
            total = total + part.astype(jnp.bfloat16).astype(jnp.float32)
        outputs.append(total.astype(jnp.bfloat16))
    result = jnp.stack(outputs, axis=1)
    returned = core_and_chips(result, (("expert_0", "expert_1"), "expert_2"), (1, 0), 0, 1)
    picked = returned[slots, final]
    return (gate[:, None] * picked.astype(jnp.float32)).astype(jnp.bfloat16)


def solution(mesh):
    torus = Mesh(
        mesh.devices.reshape(4, 4, 2, mesh.shape["helper"]),
        ("expert_0", "expert_1", "expert_2", "helper"),
    )
    in_specs = (
        P(EXPERT_HELPER, None),
        P(EXPERT_HELPER),
        P(EXPERT_HELPER, None),
        P(EXPERT_HELPER, None),
        P(),
        P(EXPERT, None, "helper"),
        P(EXPERT, "helper", None),
    )
    out_specs = P(EXPERT_HELPER, None)
    return jax.shard_map(
        on_device, mesh=torus, in_specs=in_specs, out_specs=out_specs, check_vma=False
    )
```

profile of v0, /device:TPU:0, one launch (start us, length us, event | category | flops | bytes accessed | tf_op | source)
XLA Modules:
  0.0 539.2 jit_solution(8515442696640882063)
XLA Ops:
  6.5 0.7 all-gather.3.cloned.1.call-update
  7.3 0.7 all-gather.5.cloned.1.call-update
  10.6 8.9 %scatter_custom_fusion = bf16[3072,768]{1,0:T(8,128)(2,1)} fusion(s32[1024]{0:T(1024)S(1)} %broadcast_select_fusion, bf16[1024,768]{1,0:T(8,128)(2,1)} %param.7, bf16[]{:T(256)} %constant.31.clone.1), kind=kCustom, calls=%fused_computation.4 | custom fusion | bytes 4719104
  19.5 9.4 %reshape.114 = bf16[24,32,4,768]{3,2,1,0:T(4,128)(2,1)} reshape(bf16[3072,768]{1,0:T(8,128)(2,1)} %scatter_custom_fusion) | data formatting | bytes 9437184 | tf_op jit(solution)/shard_map/reshape | solution.py:13
  28.9 6.7 %copy.35 = bf16[24,32,4,768]{3,0,2,1:T(8,128)(2,1)S(1)} copy(bf16[24,32,4,768]{3,2,1,0:T(4,128)(2,1)} %reshape.114) | data formatting | bytes 9437184 | tf_op jit(solution)/shard_map/reshape | solution.py:13
  35.9 7.5 %all_to_all.20 = bf16[16,2,24,4,768]{4,2,0,3,1:T(8,128)(2,1)S(1)} all-to-all(bf16[16,2,24,4,768]{4,2,0,3,1:T(8,128)(2,1)S(1)} %copy.36), channel_id=1, replica_groups=mesh['expert_0'=4,'expert_1'=4,'expert_2'=2,'helper'=4] {'expert_2'}, dimensions={1} | all-to-all | bytes 9437184 | tf_op jit(solution)/shard_map/all_to_all | solution.py:27
  43.9 64.7 %all_to_all.21 = bf16[16,2,24,4,768]{4,2,1,3,0:T(8,128)(2,1)S(1)} all-to-all(bf16[16,2,24,4,768]{4,2,1,3,0:T(8,128)(2,1)S(1)} %copy.37), channel_id=1, replica_groups=mesh['expert_0'=4,'expert_1'=4,'expert_2'=2,'helper'=4] {'expert_0','exp..., dimensions={0} | all-to-all | bytes 9437184 | tf_op jit(solution)/shard_map/all_to_all | solution.py:27
  108.6 2.5 copy.38
  111.1 72.8 %all-gather.3.cloned.1.call-done = bf16[4,768,3072]{2,1,0:T(8,128)(2,1)} async-done(((bf16[4,768,768]{2,1,0:T(8,128)(2,1)}), bf16[4,768,3072]{2,1,0:T(8,128)(2,1)}) %all-gather.3.cloned.1.call-update) | async-done | bytes 18874384 | tf_op jit(solution)/shard_map/all_gather | solution.py:70
  183.9 173.4 %all-gather.5.cloned.1.call-done = bf16[4,3072,768]{2,1,0:T(8,128)(2,1)} async-done(((bf16[4,768,768]{2,1,0:T(8,128)(2,1)}), bf16[4,3072,768]{2,1,0:T(8,128)(2,1)}) %all-gather.5.cloned.1.call-update) | async-done | bytes 18874384 | tf_op jit(solution)/shard_map/all_gather | solution.py:71
  357.3 4.1 convolution_convert_fusion.2
  361.4 5.1 convolution_convert_fusion.1
  366.5 5.1 convolution_convert_fusion
  371.7 4.1 convolution_convert_fusion.6
  375.8 5.1 convolution_convert_fusion.5
  380.9 5.2 convolution_convert_fusion.4
  386.1 5.1 convolution_convert_fusion.10
  391.2 5.4 convolution_convert_fusion.9
  396.6 5.2 convolution_convert_fusion.8
  401.7 5.1 convolution_convert_fusion.14
  406.8 5.1 convolution_convert_fusion.13
  412.0 5.1 convolution_convert_fusion.12
  417.1 4.9 add_convert_fusion
  422.0 4.9 add_convert_fusion.1
  427.0 5.2 add_convert_fusion.2
  432.2 6.6 %add_convert_fusion.3 = bf16[768,768]{1,0:T(8,128)(2,1)} fusion(bf16[768,768]{1,0:T(8,128)(2,1)} %convolution_convert_fusion.12, bf16[768,768]{1,0:T(8,128)(2,1)} %convolution_convert_fusion.13, bf16[768,768]{1,0:T(8,128)(2,1)} %convolution_convert_fusion.14, bf16[4,3072,768]{2,1,0:T(8,128)(2,1)} %all-gather.5.cloned.1.call-done, ...), kind=kOutput, calls=%fused_computation.21 | convolution fusion | flops 1818427392 | bytes 8257536 | tf_op jit(solution)/shard_map/dot_general | solution.py:56
  438.7 1.7 pad_maximum_fusion
  440.8 7.5 %all_to_all.22 = bf16[16,2,24,4,768]{4,2,0,3,1:T(8,128)(2,1)S(1)} all-to-all(bf16[16,2,24,4,768]{4,2,0,3,1:T(8,128)(2,1)S(1)} %copy.46), channel_id=1, replica_groups=mesh['expert_0'=4,'expert_1'=4,'expert_2'=2,'helper'=4] {'expert_2'}, dimensions={1} | all-to-all | bytes 9437184 | tf_op jit(solution)/shard_map/all_to_all | solution.py:27
  448.8 63.6 %all_to_all.23 = bf16[16,2,24,4,768]{4,2,1,3,0:T(8,128)(2,1)S(1)} all-to-all(bf16[16,2,24,4,768]{4,2,1,3,0:T(8,128)(2,1)S(1)} %copy.43), channel_id=1, replica_groups=mesh['expert_0'=4,'expert_1'=4,'expert_2'=2,'helper'=4] {'expert_0','exp..., dimensions={0} | all-to-all | bytes 9437184 | tf_op jit(solution)/shard_map/all_to_all | solution.py:27
  512.9 3.2 copy.47
  516.1 14.3 %gather_fusion = bf16[1024,768]{1,0:T(8,128)(2,1)S(1)} fusion(bf16[24,128,768]{2,1,0:T(8,128)(2,1)} %copy.47, s32[1024]{0:T(1024)S(1)} %bitcast.231), kind=kCustom, calls=%fused_computation | custom fusion | bytes 3153920 | tf_op jit(solution)/shard_map/gather | solution.py:87
  530.3 1.5 multiply_convert_fusion
  (42 shorter events, 4.7 us)
Async XLA Ops:
  6.5 177.4 %all-gather.3.cloned.1.call-start = ((), (), s32[]{:S(2)}) async-start(), calls=%async_computation.4 | async-start | bytes 23592960 | tf_op jit(solution)/shard_map/all_gather | solution.py:70
  7.3 0.8 copy-start.1
  7.3 0.9 copy-start
  7.3 350.0 %all-gather.5.cloned.1.call-start = ((), (), s32[]{:S(2)}) async-start(), calls=%async_computation.5 | async-start | bytes 23592960 | tf_op jit(solution)/shard_map/all_gather | solution.py:71
  8.0 0.7 copy-start.3
  8.5 1.9 copy-start.5
  8.6 1.9 copy-start.4
  516.1 14.3 %copy-start.2 = (f32[1024]{0:T(1024)S(1)}, f32[1024]{0:T(1024)}, u32[]{:S(2)}) copy-start(f32[1024]{0:T(1024)} %param.8) | copy-start | bytes 12292
Sparse Core Ops, SparseCore 0:
  9.0 174.8 all-gather.2
  185.6 171.6 all-gather.4
where the time goes:
time: 545 us; the launch traced here: 539 us
  waiting for transfers between devices  248 us (46%)
  blocking collectives  143 us (26%)
  matrix products  81.4 us (15%)
  local copies, waits for them, and re-layouts  47.6 us (9%)
  between operations  14.2 us (3%)
    all_gather x1, waiting for transfers between devices, on_device(): lax.all_gather(w_out, 'helper', axis=1, tiled=True)  173 us
    all_to_all x4, blocking collectives, exchange_in_order(): lax.all_to_all(parts, axes[k], split_axis=k, concat_axis=k, tiled=True)  143 us
    dot_general x16, matrix products, quarter_term(): return jnp.dot(hidden, weight_out, preferred_element_type=jnp.float32)  81.4 us
    all_gather x1, waiting for transfers between devices, on_device(): lax.all_gather(w_in, 'helper', axis=2, tiled=True)  72.8 us
    reshape x2, local copies, waits for them, and re-layouts, split_up(): parts = array.reshape(*dims[:dim], size, dims[dim] // size, *dims[dim + 1:])  16 us
    gather x1, local copies, waits for them, and re-layouts, on_device(): picked = returned[slots, final]  14.3 us
  transfers between devices with their start and end apart: 2, of which 2 were waited for; matrix products, arithmetic and copies ran while one was open for 6% of the time, Pallas kernels for 0%

commit v1 on v0

v1 whole, which is shorter than its diff:
```python
import functools

import jax
import jax.numpy as jnp
from jax import lax
from jax.experimental import pallas as pl
from jax.experimental.pallas import tpu as pltpu
from jax.sharding import Mesh
from jax.sharding import PartitionSpec as P

EXPERT = ("expert_0", "expert_1", "expert_2")
EXPERT_HELPER = ("expert_0", "expert_1", "expert_2", "helper")
BIN = 64
ROOM = 512
PAIR_A = [(0, 1), (1, 0), (2, 3), (3, 2)]
PAIR_B = [(1, 2), (2, 1), (3, 0), (0, 3)]
F32 = jnp.float32
BF16 = jnp.bfloat16
VMEM_LIMIT = 24 * 1024 * 1024


def dot(a, b):
    return jnp.dot(a, b, preferred_element_type=F32)


def dot_nt(a, b):
    return lax.dot_general(a, b, (((1,), (1,)), ((), ())), preferred_element_type=F32)


def iota(shape, dim):
    return lax.broadcasted_iota(jnp.int32, shape, dim)


def ones_where(cond):
    return jnp.where(cond, 1.0, 0.0).astype(BF16)


def params():
    return pltpu.CompilerParams(vmem_limit_bytes=VMEM_LIMIT)


def cost(flops, read):
    return pl.CostEstimate(flops=flops, bytes_accessed=read, transcendentals=0)


def route_kernel(held, first_ref, backup_ref, cap_ref, gate_ref, row_ref, col_ref, count_ref):
    count = cap_ref.shape[1]
    toks = first_ref.shape[1]
    lanes = iota((count, toks), 0)
    first = first_ref[...]
    backup = backup_ref[...]
    one = jnp.where(lanes == first, 1.0, 0.0)
    two = jnp.where(lanes == backup, 1.0, 0.0)
    earlier = ones_where(iota((toks, toks), 0) < iota((toks, toks), 1))
    rank = jnp.sum(dot(one.astype(BF16), earlier) * one, axis=0, keepdims=True)
    cap = jnp.broadcast_to(cap_ref[...].astype(F32), (8, count)).astype(BF16)
    limit = dot(cap, one.astype(BF16))[0:1]
    kept = jnp.where(rank < limit, 1.0, 0.0)
    spill = two * (1.0 - kept)
    spill_rank = jnp.sum(dot(spill.astype(BF16), earlier) * spill, axis=0, keepdims=True)
    mine = one * kept
    n_kept = jnp.sum(mine, axis=1, keepdims=True)
    final = mine + spill
    n_all = jnp.sum(final, axis=1, keepdims=True)
    e0, e1 = iota((count, count), 0), iota((count, count), 1)
    before = ones_where((e1 < e0) & (e1 // held == e0 // held))
    start = dot(before, jnp.broadcast_to(n_all, (count, count)).astype(BF16))[:, 0:1]
    place = jnp.sum(final * start + spill * n_kept, axis=0, keepdims=True)
    place = place + jnp.where(kept > 0.5, rank, spill_rank)
    owner = jnp.where(kept > 0.5, first, backup) // held
    row = jnp.where(place < BIN, owner.astype(F32) * BIN + place, -1.0)
    row_ref[...] = jnp.broadcast_to(row, (8, toks)).astype(jnp.int32)
    stacked = jnp.where(
        iota((128, toks), 0) == 0,
        jnp.broadcast_to(row, (128, toks)),
        jnp.broadcast_to(gate_ref[...], (128, toks)),
    )
    col_ref[...] = stacked.T
    every = jnp.ones((8, toks), BF16)
    count_ref[...] = dot_nt(every, final.astype(BF16))[0:1].astype(jnp.int32)


def route(first, backup, capacity, gate, held):
    toks, count = first.shape[1], capacity.shape[1]
    return pl.pallas_call(
        functools.partial(route_kernel, held),
        out_shape=(
            jax.ShapeDtypeStruct((8, toks), jnp.int32),
            jax.ShapeDtypeStruct((toks, 128), F32),
            jax.ShapeDtypeStruct((1, count), jnp.int32),
        ),
        compiler_params=params(),
        cost_estimate=cost(4 * toks * toks * count, toks * 512),
        name="route",
    )(first, backup, capacity, gate)


def pick_kernel(first, index_ref, rows_ref, out_ref):
    count, many = out_ref.shape[0], rows_ref.shape[0]
    here = iota((count, many), 0) + (first + pl.program_id(0) * count)
    out_ref[...] = dot(ones_where(here == index_ref[0:1, :]), rows_ref[...]).astype(BF16)


def pick(index, rows, first, count, blocks, name):
    many, wide = rows.shape
    block = count // blocks
    return pl.pallas_call(
        functools.partial(pick_kernel, first),
        out_shape=jax.ShapeDtypeStruct((count, wide), BF16),
        grid=(blocks,),
        in_specs=[
            pl.BlockSpec((8, many), lambda i: (0, 0)),
            pl.BlockSpec((many, wide), lambda i: (0, 0)),
        ],
        out_specs=pl.BlockSpec((block, wide), lambda i: (i, 0)),
        compiler_params=params(),
        cost_estimate=cost(2 * count * many * wide, 2 * (count + many) * wide),
        name=name,
    )(index, rows)


def places_kernel(held, group_ref, counts_ref, row_ref, col_ref, over_ref):
    sources, count = counts_ref.shape
    total = sources * BIN
    counts = counts_ref[...].astype(F32).astype(BF16)
    fullest = jnp.max(dot(counts, ones_where(iota((count, count), 0) // held == iota((count, count), 1))))
    busiest = jnp.max(dot(jnp.ones((8, sources), BF16), counts))
    over = jnp.where((fullest > BIN) | (busiest > ROOM), 1, 0)
    over_ref[...] = jnp.broadcast_to(over, (8, 128))
    which = iota((8, count), 0)
    mine = ones_where((iota((8, count), 1) == group_ref[0] * held + which) & (which < held))
    n = dot_nt(mine, counts)
    base = dot(n.astype(BF16), ones_where(iota((sources, sources), 0) < iota((sources, sources), 1)))
    begin = jnp.zeros((8, sources), F32)
    for j in range(held):
        ahead = iota((8, sources), 0) > j
        begin = begin + jnp.where(ahead, jnp.broadcast_to(n[j : j + 1], (8, sources)), 0.0)
    shift = base - begin + 128.0
    high = jnp.floor(shift * (1.0 / 128.0))
    low = shift - high * 128.0
    spread = ones_where(iota((sources, total), 1) // BIN == iota((sources, total), 0))
    place = dot(high.astype(BF16), spread) * 128.0 + dot(low.astype(BF16), spread) - 128.0
    begin = dot(begin.astype(BF16), spread)
    end = begin + dot(n.astype(BF16), spread)
    r = (iota((8, total), 1) % BIN).astype(F32)
    place = place + r
    inside = (r >= begin) & (r < end) & (place < ROOM)
    index = jnp.where(inside, place + iota((8, total), 0).astype(F32) * ROOM + 1.0, 0.0)
    index = jnp.sum(index, axis=0, keepdims=True) - 1.0
    row_ref[...] = jnp.broadcast_to(index, (8, total)).astype(jnp.int32)
    col_ref[...] = jnp.broadcast_to(index, (128, total)).T


def places(group, counts, held):
    total = counts.shape[0] * BIN
    return pl.pallas_call(
        functools.partial(places_kernel, held),
        out_shape=(
            jax.ShapeDtypeStruct((8, total), jnp.int32),
            jax.ShapeDtypeStruct((total, 128), F32),
            jax.ShapeDtypeStruct((8, 128), jnp.int32),
        ),
        in_specs=[
            pl.BlockSpec(memory_space=pltpu.SMEM),
            pl.BlockSpec(memory_space=pltpu.VMEM),
        ],
        compiler_params=params(),
        cost_estimate=cost(1 << 27, 1 << 20),
        name="places",
    )(group, counts)


def expert_kernel(steps, rows_ref, in0_ref, out0_ref, in1_ref, out1_ref, part_ref, total_ref):
    k = pl.program_id(0)

    def term(in_ref, out_ref):
        hidden = jnp.maximum(dot(rows_ref[...], in_ref[0]), 0.0).astype(BF16)
        return dot(hidden, out_ref[0])

    @pl.when(k == 0)
    def _():
        total_ref[...] = term(in0_ref, out0_ref)

    @pl.when((k > 0) & (k < steps))
    def _():
        total_ref[...] += term(in0_ref, out0_ref)

    @pl.when((k >= steps) & (k < 2 * steps - 1))
    def _():
        total_ref[...] += term(in1_ref, out1_ref)

    @pl.when(k == 2 * steps - 1)
    def _():
        part_ref[...] = (total_ref[...] + term(in1_ref, out1_ref)).astype(part_ref.dtype)


def expert(rows, w_in, w_out, other, j, dtype):
    room, wide = rows.shape
    half = other.shape[0] // 2
    hid = w_in.shape[2]
    steps = 2
    piece = hid // steps
    own, theirs = lambda k: jnp.minimum(k, steps - 1), lambda k: jnp.maximum(k - steps, 0)
    return pl.pallas_call(
        functools.partial(expert_kernel, steps),
        out_shape=jax.ShapeDtypeStruct((room, wide), dtype),
        grid=(2 * steps,),
        in_specs=[
            pl.BlockSpec((room, wide), lambda k: (0, 0)),
            pl.BlockSpec((1, wide, piece), lambda k: (j, 0, own(k))),
            pl.BlockSpec((1, piece, wide), lambda k: (j, own(k), 0)),
            pl.BlockSpec((1, wide, piece), lambda k: (j % half, 0, theirs(k))),
            pl.BlockSpec((1, piece, wide), lambda k: (half + j % half, theirs(k), 0)),
        ],
        out_specs=pl.BlockSpec((room, wide), lambda k: (0, 0)),
        scratch_shapes=[pltpu.VMEM((room, wide), F32)],
        compiler_params=params(),
        cost_estimate=cost(8 * room * wide * hid, 8 * wide * hid + 6 * room * wide),
        name="expert",
    )(rows, w_in, w_out, other, other)


def back_kernel(held, col_ref, *refs):
    own, other, out_ref = refs[:held], refs[held : 2 * held], refs[2 * held]
    rows = out_ref.shape[0]
    col = col_ref[:, 0:1].astype(jnp.int32)
    total = None
    for j in range(held):
        value = (own[j][...] + other[j][...].astype(F32)).astype(BF16)
        pick = ones_where(col - j * ROOM == iota((rows, ROOM), 1))
        part = dot(pick, value)
        total = part if total is None else total + part
    out_ref[...] = total.astype(BF16)


def back(col, own, other):
    held = len(own)
    total, wide = col.shape[0], own[0].shape[1]
    block = 512
    whole = pl.BlockSpec((ROOM, wide), lambda i: (0, 0))
    return pl.pallas_call(
        functools.partial(back_kernel, held),
        out_shape=jax.ShapeDtypeStruct((total, wide), BF16),
        grid=(total // block,),
        in_specs=[pl.BlockSpec((block, 128), lambda i: (i, 0))] + [whole] * (2 * held),
        out_specs=pl.BlockSpec((block, wide), lambda i: (i, 0)),
        compiler_params=params(),
        cost_estimate=cost(2 * total * held * ROOM * wide, 8 * total * wide),
        name="back",
    )(col, *own, *other)


def combine_kernel(col_ref, returned_ref, out_ref):
    rows, total = out_ref.shape[0], returned_ref.shape[0]
    col = col_ref[:, 0:1].astype(jnp.int32)
    gate = col_ref[:, 1:2]
    pick = ones_where(col == iota((rows, total), 1))
    out_ref[...] = (gate * dot(pick, returned_ref[...])).astype(BF16)


def combine(col, returned):
    toks = col.shape[0]
    total, wide = returned.shape
    block = 256
    return pl.pallas_call(
        combine_kernel,
        out_shape=jax.ShapeDtypeStruct((toks, wide), BF16),
        grid=(toks // block,),
        in_specs=[
            pl.BlockSpec((block, 128), lambda i: (i, 0)),
            pl.BlockSpec((total, wide), lambda i: (0, 0)),
        ],
        out_specs=pl.BlockSpec((block, wide), lambda i: (i, 0)),
        compiler_params=params(),
        cost_estimate=cost(2 * total * toks * wide, 4 * total * wide),
        name="combine",
    )(col, returned)


def assign(first, backup, capacity, count, slot):
    columns = jnp.arange(count, dtype=jnp.int32)
    where = jnp.arange(first.shape[0], dtype=jnp.int32)
    earlier = ones_where(where[None, :] < where[:, None])
    onehot = (first[:, None] == columns[None, :]).astype(F32)
    rank = jnp.sum(dot(earlier, onehot.astype(BF16)) * onehot, axis=1)
    limit = jnp.sum(onehot * capacity[None, :].astype(F32), axis=1)
    kept = rank < limit
    spill = jnp.where((backup[:, None] == columns[None, :]) & ~kept[:, None], 1.0, 0.0)
    spill_rank = jnp.sum(dot(earlier, spill.astype(BF16)) * spill, axis=1)
    final = jnp.where(kept, first, backup)
    slots = jnp.where(kept, rank, slot + spill_rank).astype(jnp.int32)
    return slots, final


def general(tokens, gate, first, backup, capacity, w_in, w_out):
    held = w_in.shape[0]
    owners = lax.axis_size(EXPERT)
    helpers = lax.axis_size("helper")
    experts = held * owners
    slot = max(6, 3 * tokens.shape[0] // (2 * experts))
    slots, final = assign(first, backup, capacity, experts, slot)
    wide = tokens.shape[1]
    buffer = jnp.zeros((experts, 2 * slot, wide), BF16).at[final, slots].set(tokens)
    buffer = buffer.reshape(owners, held * 2 * slot, wide)
    arrived = lax.all_to_all(buffer, EXPERT, 0, 0, tiled=True)
    arrived = arrived.reshape(owners, held, 2 * slot, wide)
    whole_in = lax.all_gather(w_in, "helper", axis=2, tiled=True)
    whole_out = lax.all_gather(w_out, "helper", axis=1, tiled=True)
    width = whole_in.shape[2] // helpers
    outputs = []
    for e in range(held):
        rows = arrived[:, e].reshape(owners * 2 * slot, wide)
        total = jnp.zeros(rows.shape, F32)
        for q in range(helpers):
            part = slice(q * width, (q + 1) * width)
            hidden = jnp.maximum(dot(rows, whole_in[e, :, part]), 0.0).astype(BF16)
            total = total + dot(hidden, whole_out[e, part, :]).astype(BF16).astype(F32)
        outputs.append(total.astype(BF16).reshape(owners, 2 * slot, wide))
    result = jnp.stack(outputs, axis=1).reshape(owners, held * 2 * slot, wide)
    returned = lax.all_to_all(result, EXPERT, 0, 0, tiled=True)
    picked = returned.reshape(experts, 2 * slot, wide)[final, slots]
    return (gate[:, None] * picked.astype(F32)).astype(BF16)


def on_device(tokens, gate, expert_ids, backup_ids, capacity, w_in, w_out):
    held = w_in.shape[0]
    owners = lax.axis_size(EXPERT)
    helpers = lax.axis_size("helper")
    toks, wide = tokens.shape
    half = held // 2
    pairs = [PAIR_A if j < half else PAIR_B for j in range(held)]
    cross = [PAIR_B if j < half else PAIR_A for j in range(held)]
    order = [k for i in range(half) for k in (i, i + half)]
    group = lax.axis_index(EXPERT).astype(jnp.int32).reshape(1)
    pieces = [jnp.concatenate([w_in[k : k + half], w_out[k : k + half]]) for k in (0, half)]
    pieces, expert_ids = lax.optimization_barrier((pieces, expert_ids))
    other = [lax.ppermute(p, "helper", pairs[k * half]) for k, p in enumerate(pieces)]
    row, col, count = route(
        expert_ids.reshape(1, toks),
        backup_ids.reshape(1, toks),
        capacity.reshape(1, -1),
        gate.reshape(1, toks),
        held,
    )
    counts = lax.all_gather(count, EXPERT, axis=0, tiled=True)
    row, counts = lax.optimization_barrier((row, counts))
    bins = pick(row, tokens, 0, owners * BIN, 4, "dispatch")
    arrived = lax.all_to_all(bins.reshape(owners, BIN, wide), EXPERT, 0, 0, tiled=True)
    arrived = arrived.reshape(owners * BIN, wide)
    place_row, place_col, over = places(group, counts, held)
    overs = [over] + [
        lax.ppermute(over, "helper", [(i, (i + k) % helpers) for i in range(helpers)])
        for k in range(1, helpers)
    ]
    rows, theirs = {}, {}
    for j in order:
        rows[j] = pick(place_row, arrived, j * ROOM, ROOM, 1, "regroup")
        theirs[j] = lax.ppermute(rows[j], "helper", cross[j])
    own, sent = {}, {}
    for j in order:
        args = (w_in, w_out, other[j // half], j)
        own[j] = expert(rows[j], *args, F32)
        sent[j] = lax.ppermute(expert(theirs[j], *args, BF16), "helper", cross[j])
    result = back(place_col, [own[j] for j in range(held)], [sent[j] for j in range(held)])
    returned = lax.all_to_all(result.reshape(owners, BIN, wide), EXPERT, 0, 0, tiled=True)
    mixed = combine(col, returned.reshape(owners * BIN, wide))
    return lax.cond(
        functools.reduce(jnp.maximum, [o[0, 0] for o in overs]) > 0,
        lambda ops: general(*ops[1:]),
        lambda ops: ops[0],
        (mixed, tokens, gate, expert_ids[:, 0], backup_ids[:, 0], capacity, w_in, w_out),
    )


def solution(mesh):
    torus = Mesh(
        mesh.devices.reshape(4, 4, 2, mesh.shape["helper"]),
        ("expert_0", "expert_1", "expert_2", "helper"),
    )
    in_specs = (
        P(EXPERT_HELPER, None),
        P(EXPERT_HELPER),
        P(EXPERT_HELPER, None),
        P(EXPERT_HELPER, None),
        P(),
        P(EXPERT, None, "helper"),
        P(EXPERT, "helper", None),
    )
    out_specs = P(EXPERT_HELPER, None)
    return jax.shard_map(
        on_device, mesh=torus, in_specs=in_specs, out_specs=out_specs, check_vma=False
    )
```

time: 545 us -> 289 us (0.53)
  waiting for transfers between devices: 248 us -> 116 us
  blocking collectives: 143 us -> 22.9 us
  matrix products: 81.4 us -> 0 us
  Pallas kernels: 0 us -> 74.4 us
  starting transfers between devices: 0.04 us -> 37.1 us
  local copies, waits for them, and re-layouts: 47.6 us -> 11.8 us
    all_gather x2 -> x0, waiting for transfers between devices: 246 us -> none  [the longest x1 173 us: on_device(): lax.all_gather(w_out, 'helper', axis=1, tiled=True)]
    all_to_all x4 -> x0, blocking collectives: 143 us -> none  [exchange_in_order(): lax.all_to_all(parts, axes[k], split_axis=k, concat_axis=k, tiled=True)]
    dot_general x16 -> x0, matrix products: 81.4 us -> none  [quarter_term(): return jnp.dot(hidden, weight_out, preferred_element_type=jnp.float32)]
    pallas_call x0 -> x17, Pallas kernels: none -> 74.4 us  [the longest x8 48.2 us: expert(): pl.pallas_call(functools.partial(expert_kernel, steps), out_shape=jax.Sha...]
    all_to_all x0 -> x2, waiting for transfers between devices: none -> 72.7 us  [the longest x1 40 us: on_device(): lax.all_to_all(bins.reshape(owners, BIN, wide), EXPERT, 0, 0, tiled=True)]
    ppermute x0 -> x13, waiting for transfers between devices: none -> 43.5 us  [the longest x4 42.6 us: on_device(): theirs[j] = lax.ppermute(rows[j], 'helper', cross[j])]
    ppermute x0 -> x13, starting transfers between devices: none -> 23.2 us  [the longest x4 12.6 us: on_device(): sent[j] = lax.ppermute(expert(theirs[j], *args, BF16), 'helper', cross[j])]
    all_gather x0 -> x1, blocking collectives: none -> 22.9 us  [on_device(): counts = lax.all_gather(count, EXPERT, axis=0, tiled=True)]
  transfers between devices with their start and end apart: 2 -> 15, of which waited for: 2 -> 5; matrix products, arithmetic and copies ran while one was open for 6% -> 1% of each run, Pallas kernels for 0% -> 22%
where the time goes in v1:
time: 289 us; the launch traced here: 284 us
  waiting for transfers between devices  116 us (40%)
  Pallas kernels  74.4 us (26%)
  starting transfers between devices  37.1 us (13%)
  blocking collectives  22.9 us (8%)
  between operations  16.6 us (6%)
  local copies, waits for them, and re-layouts  11.8 us (4%)
  other arithmetic  3.98 us (1%)
    pallas_call x8, Pallas kernels, expert(): pl.pallas_call(functools.partial(expert_kernel, steps), out_shape=jax.Sha...  48.2 us
    ppermute x4, waiting for transfers between devices, on_device(): theirs[j] = lax.ppermute(rows[j], 'helper', cross[j])  42.6 us
    all_to_all x1, waiting for transfers between devices, on_device(): lax.all_to_all(bins.reshape(owners, BIN, wide), EXPERT, 0, 0, tiled=True)  40 us
    all_to_all x1, waiting for transfers between devices, on_device(): lax.all_to_all(result.reshape(owners, BIN, wide), EXPERT, 0, 0, tiled=True)  32.7 us
    all_gather x1, blocking collectives, on_device(): counts = lax.all_gather(count, EXPERT, axis=0, tiled=True)  22.9 us
    ppermute x4, starting transfers between devices, on_device(): sent[j] = lax.ppermute(expert(theirs[j], *args, BF16), 'helper', cross[j])  12.6 us
    pallas_call x5, Pallas kernels, pick(): pl.pallas_call(functools.partial(pick_kernel, first), out_shape=jax.Shape...  11.2 us
    pallas_call x1, Pallas kernels, back(): pl.pallas_call(functools.partial(back_kernel, held), out_shape=jax.ShapeD...  8.7 us
  transfers between devices with their start and end apart: 15, of which 5 were waited for; matrix products, arithmetic and copies ran while one was open for 1% of the time, Pallas kernels for 22%

profile of v1, /device:TPU:0, one launch (start us, length us, event | category | flops | bytes accessed | tf_op | source)
XLA Modules:
  0.0 284.0 jit_solution(7545425338060995612)
XLA Ops:
  6.5 2.8 fusion.40
  10.7 4.0 %pad_maximum_fusion.1 = (bf16[4,768,768]{2,1,0:T(8,128)(2,1)}, bf16[4,768,768]{2,1,0:T(8,128)(2,1)}) fusion(bf16[2,768,768]{2,1,0:T(8,128)(2,1)S(1)} %get-tuple-element.67, bf16[2,768,768]{2,1,0:T(8,128)(2,1)S(1)} %get-tuple-element.65, bf16[2,768,768]{2,1,0:T(8,128)(2,1)S(1)} %get-tuple-element.66, bf16[2,768,768]{2,1,0:T(8,128)(2,1)S(1)} %get-tuple-element.64), kind=kLoop, calls=%fused_computation.129 | loop fusion | flops 4718592 | bytes 18874368 | tf_op jit(solution)/shard_map/concatenate | solution.py:335
  14.6 2.8 %collective-permute-start.4 = (bf16[4,768,768]{2,1,0:T(8,128)(2,1)}, bf16[4,768,768]{2,1,0:T(8,128)(2,1)}, u32[]{:S(2)}, u32[]{:S(2)}) collective-permute-start(bf16[4,768,768]{2,1,0:T(8,128)(2,1)} %get-tuple-element.55), channel_id=1, source_target_pairs={{1,2},{2,1},{3,0},{0,3},{5,6},{6,5},{7,4},{4,7},{9,10},{10,9},{11,... | collective-permute-start | bytes 14155784 | tf_op jit(solution)/shard_map/ppermute | solution.py:337
  17.7 1.3 route.1
  19.8 22.9 %all-gather = s32[32,1,128]{2,1,0:T(1,128)S(1)} all-gather(s32[1,1,128]{2,1,0:T(1,128)S(1)} %bitcast.197), channel_id=1, replica_groups=mesh['expert_0'=4,'expert_1'=4,'expert_2'=2,'helper'=4] {'expert_0','exp..., dimensions={0}, use_global_device_ids=true | all-gather | bytes 16896 | tf_op jit(solution)/shard_map/all_gather | solution.py:345
  42.7 4.0 %dispatch.1 = bf16[2048,768]{1,0:T(8,128)(2,1)S(1)} custom-call(s32[8,1024]{1,0:T(8,128)S(1)} %get-tuple-element.53.index_ref, bf16[1024,768]{1,0:T(8,128)(2,1)S(1)} %copy-done.13), custom_call_target="tpu_custom_call" | custom-call | flops 3221225472 | bytes 4718592 | tf_op jit(solution)/shard_map/dispatch/pallas_call | solution.py:107
  46.7 1.7 copy-done
  48.4 5.5 %all-to-all-start.2 = ((bf16[32,64,768]{2,1,0:T(8,128)(2,1)}), bf16[32,64,768]{2,1,0:T(8,128)(2,1)S(1)}, u32[]{:S(2)}, u32[]{:S(2)}) async-start(bf16[32,64,768]{2,1,0:T(8,128)(2,1)} %bitcast.195), calls=%async_computation.2 | async-start | bytes 6291456 | tf_op jit(solution)/shard_map/all_to_all | solution.py:348
  55.7 40.0 %all-to-all-done.2 = bf16[32,64,768]{2,1,0:T(8,128)(2,1)S(1)} async-done(((bf16[32,64,768]{2,1,0:T(8,128)(2,1)}), bf16[32,64,768]{2,1,0:T(8,128)(2,1)S(1)}, u32[]{:S(2)}, u32[]{:S(2)}) %all-to-all-start.2) | async-done | bytes 3145760 | tf_op jit(solution)/shard_map/all_to_all | solution.py:348
  95.7 1.8 regroup.7.rows_ref
  97.5 1.9 collective-permute-start.11
  99.4 1.8 regroup.6.rows_ref
  101.5 1.8 regroup.5.rows_ref
  103.3 1.2 collective-permute-start.7
  104.5 1.8 regroup.4.rows_ref
  106.3 32.9 %collective-permute-done.11.rows_ref = bf16[512,768]{1,0:T(8,128)(2,1)S(1)} collective-permute-done((bf16[512,768]{1,0:T(8,128)(2,1)S(1)}, bf16[512,768]{1,0:T(8,128)(2,1)S(1)}, u32[]{:S(2)}, u32[]{:S(2)}) %collective-permute-start.11) | collective-permute-done | bytes 786464 | tf_op jit(solution)/shard_map/ppermute | solution.py:358
  140.1 6.0 %expert.15 = bf16[512,768]{1,0:T(8,128)(2,1)S(1)} custom-call(bf16[512,768]{1,0:T(8,128)(2,1)S(1)} %collective-permute-done.11.rows_ref, bf16[4,768,768]{2,1,0:T(8,128)(2,1)S(1)} %bitcast.199, bf16[4,768,768]{2,1,0:T(8,128)(2,1)S(1)} %bitcast.201, bf16[4,768,768]{2,1,0:T(8,128)(2,1)} %collective-permute-done.4.in1_ref.out1_ref, ...), custom_call_target="tpu_custom_call" | custom-call | flops 2415919104 | bytes 7077888 | tf_op jit(solution)/shard_map/expert/pallas_call | solution.py:204
  146.5 9.6 %collective-permute-done.9.rows_ref = bf16[512,768]{1,0:T(8,128)(2,1)S(1)} collective-permute-done((bf16[512,768]{1,0:T(8,128)(2,1)S(1)}, bf16[512,768]{1,0:T(8,128)(2,1)S(1)}, u32[]{:S(2)}, u32[]{:S(2)}) %collective-permute-start.9) | collective-permute-done | bytes 786464 | tf_op jit(solution)/shard_map/ppermute | solution.py:358
  156.1 6.0 %expert.14 = bf16[512,768]{1,0:T(8,128)(2,1)S(1)} custom-call(bf16[512,768]{1,0:T(8,128)(2,1)S(1)} %collective-permute-done.9.rows_ref, bf16[4,768,768]{2,1,0:T(8,128)(2,1)S(1)} %bitcast.199, bf16[4,768,768]{2,1,0:T(8,128)(2,1)S(1)} %bitcast.201, bf16[4,768,768]{2,1,0:T(8,128)(2,1)} %collective-permute-done.4.in1_ref.out1_ref, ...), custom_call_target="tpu_custom_call" | custom-call | flops 2415919104 | bytes 7077888 | tf_op jit(solution)/shard_map/expert/pallas_call | solution.py:204
  162.4 6.0 %expert.13 = bf16[512,768]{1,0:T(8,128)(2,1)S(1)} custom-call(bf16[512,768]{1,0:T(8,128)(2,1)S(1)} %collective-permute-done.7.rows_ref, bf16[4,768,768]{2,1,0:T(8,128)(2,1)S(1)} %bitcast.199, bf16[4,768,768]{2,1,0:T(8,128)(2,1)S(1)} %bitcast.201, bf16[4,768,768]{2,1,0:T(8,128)(2,1)} %collective-permute-done.3.in1_ref.out1_ref, ...), custom_call_target="tpu_custom_call" | custom-call | flops 2415919104 | bytes 7077888 | tf_op jit(solution)/shard_map/expert/pallas_call | solution.py:204
  168.4 1.2 collective-permute-start.8
  169.6 6.0 %expert.12 = bf16[512,768]{1,0:T(8,128)(2,1)S(1)} custom-call(bf16[512,768]{1,0:T(8,128)(2,1)S(1)} %collective-permute-done.5.rows_ref, bf16[4,768,768]{2,1,0:T(8,128)(2,1)S(1)} %bitcast.199, bf16[4,768,768]{2,1,0:T(8,128)(2,1)S(1)} %bitcast.201, bf16[4,768,768]{2,1,0:T(8,128)(2,1)} %collective-permute-done.3.in1_ref.out1_ref, ...), custom_call_target="tpu_custom_call" | custom-call | flops 2415919104 | bytes 7077888 | tf_op jit(solution)/shard_map/expert/pallas_call | solution.py:204
  175.6 10.6 %collective-permute-start.6 = (bf16[512,768]{1,0:T(8,128)(2,1)S(1)}, bf16[512,768]{1,0:T(8,128)(2,1)S(1)}, u32[]{:S(2)}, u32[]{:S(2)}) collective-permute-start(bf16[512,768]{1,0:T(8,128)(2,1)S(1)} %expert.12), channel_id=1, source_target_pairs={{1,2},{2,1},{3,0},{0,3},{5,6},{6,5},{7,4},{4,7},{9,10},{10,9},{11,... | collective-permute-start | bytes 2359304 | tf_op jit(solution)/shard_map/ppermute | solution.py:363
  186.2 6.0 %expert.11.refs_3_ = f32[512,768]{1,0:T(8,128)S(1)} custom-call(bf16[512,768]{1,0:T(8,128)(2,1)S(1)} %regroup.7.rows_ref, bf16[4,768,768]{2,1,0:T(8,128)(2,1)S(1)} %bitcast.199, bf16[4,768,768]{2,1,0:T(8,128)(2,1)S(1)} %bitcast.201, bf16[4,768,768]{2,1,0:T(8,128)(2,1)} %collective-permute-done.4.in1_ref.out1_ref, ...), custom_call_target="tpu_custom_call" | custom-call | flops 2415919104 | bytes 7077888 | tf_op jit(solution)/shard_map/expert/pallas_call | solution.py:204
  192.2 6.0 %expert.10.refs_2_ = f32[512,768]{1,0:T(8,128)S(1)} custom-call(bf16[512,768]{1,0:T(8,128)(2,1)S(1)} %regroup.6.rows_ref, bf16[4,768,768]{2,1,0:T(8,128)(2,1)S(1)} %bitcast.199, bf16[4,768,768]{2,1,0:T(8,128)(2,1)S(1)} %bitcast.201, bf16[4,768,768]{2,1,0:T(8,128)(2,1)} %collective-permute-done.4.in1_ref.out1_ref, ...), custom_call_target="tpu_custom_call" | custom-call | flops 2415919104 | bytes 7077888 | tf_op jit(solution)/shard_map/expert/pallas_call | solution.py:204
  198.2 6.0 %expert.9.refs_1_ = f32[512,768]{1,0:T(8,128)S(1)} custom-call(bf16[512,768]{1,0:T(8,128)(2,1)S(1)} %regroup.5.rows_ref, bf16[4,768,768]{2,1,0:T(8,128)(2,1)S(1)} %bitcast.199, bf16[4,768,768]{2,1,0:T(8,128)(2,1)S(1)} %bitcast.201, bf16[4,768,768]{2,1,0:T(8,128)(2,1)} %collective-permute-done.3.in1_ref.out1_ref, ...), custom_call_target="tpu_custom_call" | custom-call | flops 2415919104 | bytes 7077888 | tf_op jit(solution)/shard_map/expert/pallas_call | solution.py:204
  204.2 6.4 %expert.8.refs_0_ = f32[512,768]{1,0:T(8,128)S(1)} custom-call(bf16[512,768]{1,0:T(8,128)(2,1)S(1)} %regroup.4.rows_ref, bf16[4,768,768]{2,1,0:T(8,128)(2,1)S(1)} %bitcast.199, bf16[4,768,768]{2,1,0:T(8,128)(2,1)S(1)} %bitcast.201, bf16[4,768,768]{2,1,0:T(8,128)(2,1)} %collective-permute-done.3.in1_ref.out1_ref, ...), custom_call_target="tpu_custom_call" | custom-call | flops 2415919104 | bytes 7077888 | tf_op jit(solution)/shard_map/expert/pallas_call | solution.py:204
  210.7 8.7 %back.1 = bf16[2048,768]{1,0:T(8,128)(2,1)} custom-call(f32[2048,128]{1,0:T(8,128)S(1)} %copy-done.2, f32[512,768]{1,0:T(8,128)S(1)} %expert.8.refs_0_, f32[512,768]{1,0:T(8,128)S(1)} %expert.9.refs_1_, f32[512,768]{1,0:T(8,128)S(1)} %expert.10.refs_2_, f32[512,768]{1,0:T(8,128)S(1)} %expert.11.refs_3_, bf16[512,768]{1,0:T(8,128)(2,1)S(1)} %collective-permute-done.6.refs_4_, ...), custom_call_target="tpu_custom_call" | custom-call | flops 6442450944 | bytes 12582912 | tf_op jit(solution)/shard_map/back/pallas_call | solution.py:241
  219.4 8.3 %all-to-all-start.3 = ((bf16[32,64,768]{2,1,0:T(8,128)(2,1)}), bf16[32,64,768]{2,1,0:T(8,128)(2,1)S(1)}, u32[]{:S(2)}, u32[]{:S(2)}) async-start(bf16[32,64,768]{2,1,0:T(8,128)(2,1)} %bitcast.64), calls=%async_computation.3 | async-start | bytes 6291456 | tf_op jit(solution)/shard_map/all_to_all | solution.py:365
  228.4 2.0 collective-permute-start.1
  236.8 32.7 %all-to-all-done.3 = bf16[32,64,768]{2,1,0:T(8,128)(2,1)S(1)} async-done(((bf16[32,64,768]{2,1,0:T(8,128)(2,1)}), bf16[32,64,768]{2,1,0:T(8,128)(2,1)S(1)}, u32[]{:S(2)}, u32[]{:S(2)}) %all-to-all-start.3) | async-done | bytes 3145760 | tf_op jit(solution)/shard_map/all_to_all | solution.py:365
  270.5 4.2 %combine.1 = bf16[1024,768]{1,0:T(8,128)(2,1)S(1)} custom-call(f32[1024,128]{1,0:T(8,128)S(1)} %copy-done.4, bf16[2048,768]{1,0:T(8,128)(2,1)S(1)} %bitcast.194), custom_call_target="tpu_custom_call" | custom-call | flops 3221225472 | bytes 6291456 | tf_op jit(solution)/shard_map/combine/pallas_call | solution.py:265
  (58 shorter events, 13.6 us)
Async XLA Ops:
  6.5 3.8 %copy-start.5 = (bf16[4,768,768]{2,1,0:T(8,128)(2,1)S(1)}, bf16[4,768,768]{2,1,0:T(8,128)(2,1)}, u32[]{:S(2)}) copy-start(bf16[4,768,768]{2,1,0:T(8,128)(2,1)} %out0_ref.15) | copy-start | bytes 14155780
  10.6 7.1 %copy-start.8 = (s32[1024,1]{0,1:T(1,128)S(1)}, s32[1024,1]{0,1:T(1,128)}, u32[]{:S(2)}) copy-start(s32[1024,1]{0,1:T(1,128)} %param.11) | copy-start | bytes 12292
  10.6 7.1 %copy-start.9 = (f32[1024]{0:T(1024)S(1)}, f32[1024]{0:T(1024)}, u32[]{:S(2)}) copy-start(f32[1024]{0:T(1024)} %param.10) | copy-start | bytes 12292
  10.6 7.1 %copy-start.10 = (s32[1024,1]{0,1:T(1,128)S(1)}, s32[1024,1]{0,1:T(1,128)}, u32[]{:S(2)}) copy-start(s32[1024,1]{0,1:T(1,128)} %param.12) | copy-start | bytes 12292
  10.6 7.1 %copy-start.14 = (s32[128]{0:T(128)S(1)}, s32[128]{0:T(128)}, u32[]{:S(2)}) copy-start(s32[128]{0:T(128)} %param.13) | copy-start | bytes 1540
  10.6 32.0 %copy-start.13 = (bf16[1024,768]{1,0:T(8,128)(2,1)S(1)}, bf16[1024,768]{1,0:T(8,128)(2,1)}, u32[]{:S(2)}) copy-start(bf16[1024,768]{1,0:T(8,128)(2,1)} %rows_ref.1) | copy-start | bytes 4718596
  14.6 125.4 %collective-permute-start.4 = (bf16[4,768,768]{2,1,0:T(8,128)(2,1)}, bf16[4,768,768]{2,1,0:T(8,128)(2,1)}, u32[]{:S(2)}, u32[]{:S(2)}) collective-permute-start(bf16[4,768,768]{2,1,0:T(8,128)(2,1)} %get-tuple-element.55), channel_id=1, source_target_pairs={{1,2},{2,1},{3,0},{0,3},{5,6},{6,5},{7,4},{4,7},{9,10},{10,9},{11,... | collective-permute-start | bytes 14155784 | tf_op jit(solution)/shard_map/ppermute | solution.py:337
  17.5 144.9 %collective-permute-start.3 = (bf16[4,768,768]{2,1,0:T(8,128)(2,1)}, bf16[4,768,768]{2,1,0:T(8,128)(2,1)}, u32[]{:S(2)}, u32[]{:S(2)}) collective-permute-start(bf16[4,768,768]{2,1,0:T(8,128)(2,1)} %get-tuple-element.54), channel_id=1, source_target_pairs={{0,1},{1,0},{2,3},{3,2},{4,5},{5,4},{6,7},{7,6},{8,9},{9,8},{10,11... | collective-permute-start | bytes 14155784 | tf_op jit(solution)/shard_map/ppermute | solution.py:337
  19.0 0.8 copy-start.3
  46.7 1.7 copy-start
  48.4 47.3 %all-to-all-start.2 = ((bf16[32,64,768]{2,1,0:T(8,128)(2,1)}), bf16[32,64,768]{2,1,0:T(8,128)(2,1)S(1)}, u32[]{:S(2)}, u32[]{:S(2)}) async-start(bf16[32,64,768]{2,1,0:T(8,128)(2,1)} %bitcast.195), calls=%async_computation.2 | async-start | bytes 6291456 | tf_op jit(solution)/shard_map/all_to_all | solution.py:348
  54.7 1.0 copy-start.1
  97.5 41.8 %collective-permute-start.11 = (bf16[512,768]{1,0:T(8,128)(2,1)S(1)}, bf16[512,768]{1,0:T(8,128)(2,1)S(1)}, u32[]{:S(2)}, u32[]{:S(2)}) collective-permute-start(bf16[512,768]{1,0:T(8,128)(2,1)S(1)} %regroup.7.rows_ref), channel_id=1, source_target_pairs={{0,1},{1,0},{2,3},{3,2},{4,5},{5,4},{6,7},{7,6},{8,9},{9,8},{10,11... | collective-permute-start | bytes 2359304 | tf_op jit(solution)/shard_map/ppermute | solution.py:358
  99.4 40.7 %slice-start = ((s8[4718592]{0:T(1024)(128)(4,1)}), s8[4194304]{0:T(1024)(128)(4,1)S(1)}, s32[]{:S(2)}) async-start(s8[4718592]{0:T(1024)(128)(4,1)} %bitcast.198), calls=%async_computation.6 | async-start | bytes 8388608
  99.4 40.7 %slice-start.2 = ((s8[4718592]{0:T(1024)(128)(4,1)}), s8[4194304]{0:T(1024)(128)(4,1)S(1)}, s32[]{:S(2)}) async-start(s8[4718592]{0:T(1024)(128)(4,1)} %bitcast.200), calls=%async_computation.8 | async-start | bytes 8388608
  101.2 38.9 %slice-start.1 = ((s8[4718592]{0:T(1024)(128)(4,1)}), s8[524288]{0:T(1024)(128)(4,1)S(1)}, s32[]{:S(2)}) async-start(s8[4718592]{0:T(1024)(128)(4,1)} %bitcast.198), calls=%async_computation.7 | async-start | bytes 1048576
  101.2 38.9 %slice-start.3 = ((s8[4718592]{0:T(1024)(128)(4,1)}), s8[524288]{0:T(1024)(128)(4,1)S(1)}, s32[]{:S(2)}) async-start(s8[4718592]{0:T(1024)(128)(4,1)} %bitcast.200), calls=%async_computation.9 | async-start | bytes 1048576
  101.2 54.9 %collective-permute-start.9 = (bf16[512,768]{1,0:T(8,128)(2,1)S(1)}, bf16[512,768]{1,0:T(8,128)(2,1)S(1)}, u32[]{:S(2)}, u32[]{:S(2)}) collective-permute-start(bf16[512,768]{1,0:T(8,128)(2,1)S(1)} %regroup.6.rows_ref), channel_id=1, source_target_pairs={{0,1},{1,0},{2,3},{3,2},{4,5},{5,4},{6,7},{7,6},{8,9},{9,8},{10,11... | collective-permute-start | bytes 2359304 | tf_op jit(solution)/shard_map/ppermute | solution.py:358
  103.3 59.1 %collective-permute-start.7 = (bf16[512,768]{1,0:T(8,128)(2,1)S(1)}, bf16[512,768]{1,0:T(8,128)(2,1)S(1)}, u32[]{:S(2)}, u32[]{:S(2)}) collective-permute-start(bf16[512,768]{1,0:T(8,128)(2,1)S(1)} %regroup.5.rows_ref), channel_id=1, source_target_pairs={{1,2},{2,1},{3,0},{0,3},{5,6},{6,5},{7,4},{4,7},{9,10},{10,9},{11,... | collective-permute-start | bytes 2359304 | tf_op jit(solution)/shard_map/ppermute | solution.py:358
  139.3 30.3 %collective-permute-start.5 = (bf16[512,768]{1,0:T(8,128)(2,1)S(1)}, bf16[512,768]{1,0:T(8,128)(2,1)S(1)}, u32[]{:S(2)}, u32[]{:S(2)}) collective-permute-start(bf16[512,768]{1,0:T(8,128)(2,1)S(1)} %regroup.4.rows_ref), channel_id=1, source_target_pairs={{1,2},{2,1},{3,0},{0,3},{5,6},{6,5},{7,4},{4,7},{9,10},{10,9},{11,... | collective-permute-start | bytes 2359304 | tf_op jit(solution)/shard_map/ppermute | solution.py:358
  146.1 64.5 %collective-permute-start.12 = (bf16[512,768]{1,0:T(8,128)(2,1)S(1)}, bf16[512,768]{1,0:T(8,128)(2,1)S(1)}, u32[]{:S(2)}, u32[]{:S(2)}) collective-permute-start(bf16[512,768]{1,0:T(8,128)(2,1)S(1)} %expert.15), channel_id=1, source_target_pairs={{0,1},{1,0},{2,3},{3,2},{4,5},{5,4},{6,7},{7,6},{8,9},{9,8},{10,11... | collective-permute-start | bytes 2359304 | tf_op jit(solution)/shard_map/ppermute | solution.py:363
  162.1 48.5 %collective-permute-start.10 = (bf16[512,768]{1,0:T(8,128)(2,1)S(1)}, bf16[512,768]{1,0:T(8,128)(2,1)S(1)}, u32[]{:S(2)}, u32[]{:S(2)}) collective-permute-start(bf16[512,768]{1,0:T(8,128)(2,1)S(1)} %expert.14), channel_id=1, source_target_pairs={{0,1},{1,0},{2,3},{3,2},{4,5},{5,4},{6,7},{7,6},{8,9},{9,8},{10,11... | collective-permute-start | bytes 2359304 | tf_op jit(solution)/shard_map/ppermute | solution.py:363
  168.4 42.2 %collective-permute-start.8 = (bf16[512,768]{1,0:T(8,128)(2,1)S(1)}, bf16[512,768]{1,0:T(8,128)(2,1)S(1)}, u32[]{:S(2)}, u32[]{:S(2)}) collective-permute-start(bf16[512,768]{1,0:T(8,128)(2,1)S(1)} %expert.13), channel_id=1, source_target_pairs={{1,2},{2,1},{3,0},{0,3},{5,6},{6,5},{7,4},{4,7},{9,10},{10,9},{11,... | collective-permute-start | bytes 2359304 | tf_op jit(solution)/shard_map/ppermute | solution.py:363
  175.6 35.0 %collective-permute-start.6 = (bf16[512,768]{1,0:T(8,128)(2,1)S(1)}, bf16[512,768]{1,0:T(8,128)(2,1)S(1)}, u32[]{:S(2)}, u32[]{:S(2)}) collective-permute-start(bf16[512,768]{1,0:T(8,128)(2,1)S(1)} %expert.12), channel_id=1, source_target_pairs={{1,2},{2,1},{3,0},{0,3},{5,6},{6,5},{7,4},{4,7},{9,10},{10,9},{11,... | collective-permute-start | bytes 2359304 | tf_op jit(solution)/shard_map/ppermute | solution.py:363
  204.2 6.5 %copy-start.2 = (f32[2048,128]{1,0:T(8,128)S(1)}, f32[2048,128]{1,0:T(8,128)}, u32[]{:S(2)}) copy-start(f32[2048,128]{1,0:T(8,128)} %copy-done.1) | copy-start | bytes 3145732
  219.4 50.1 %all-to-all-start.3 = ((bf16[32,64,768]{2,1,0:T(8,128)(2,1)}), bf16[32,64,768]{2,1,0:T(8,128)(2,1)S(1)}, u32[]{:S(2)}, u32[]{:S(2)}) async-start(bf16[32,64,768]{2,1,0:T(8,128)(2,1)} %bitcast.64), calls=%async_computation.3 | async-start | bytes 6291456 | tf_op jit(solution)/shard_map/all_to_all | solution.py:365
  227.7 4.9 %collective-permute-start = (s32[8,128]{1,0:T(8,128)S(1)}, s32[8,128]{1,0:T(8,128)S(1)}, u32[]{:S(2)}, u32[]{:S(2)}) collective-permute-start(s32[8,128]{1,0:T(8,128)S(1)} %get-tuple-element.49), channel_id=1, source_target_pairs={{0,1},{1,2},{2,3},{3,0},{4,5},{5,6},{6,7},{7,4},{8,9},{9,10},{10,1... | collective-permute-start | bytes 12296 | tf_op jit(solution)/shard_map/ppermute | solution.py:352
  228.4 6.1 %collective-permute-start.1 = (s32[8,128]{1,0:T(8,128)S(1)}, s32[8,128]{1,0:T(8,128)S(1)}, u32[]{:S(2)}, u32[]{:S(2)}) collective-permute-start(s32[8,128]{1,0:T(8,128)S(1)} %get-tuple-element.49), channel_id=1, source_target_pairs={{0,2},{1,3},{2,0},{3,1},{4,6},{5,7},{6,4},{7,5},{8,10},{9,11},{10,... | collective-permute-start | bytes 12296 | tf_op jit(solution)/shard_map/ppermute | solution.py:352
  230.4 5.2 %collective-permute-start.2 = (s32[8,128]{1,0:T(8,128)S(1)}, s32[8,128]{1,0:T(8,128)S(1)}, u32[]{:S(2)}, u32[]{:S(2)}) collective-permute-start(s32[8,128]{1,0:T(8,128)S(1)} %get-tuple-element.49), channel_id=1, source_target_pairs={{0,3},{1,0},{2,1},{3,2},{4,7},{5,4},{6,5},{7,6},{8,11},{9,8},{10,9... | collective-permute-start | bytes 12296 | tf_op jit(solution)/shard_map/ppermute | solution.py:352
  269.5 1.0 copy-start.4
  275.8 1.1 copy-start.15
